TPU v7x, 256 devices: a whole 4x4x8 slice. The times are simulated.
256 devices in a mesh: seq: 32 (over x, y, core), tp: 8 (over z).
Axes of the slice: x: 4, y: 4, z: 8, core: 2. Of those that a mesh axis runs over, the one named last changes fastest.
Arguments:
- hidden: bfloat16 [8192, 1024], P('seq'), may hold values from -6 to 6
- norm1_gain: float32 [1024], replicated, may hold values from 0.25 to 1.75
- w_query: bfloat16 [1024, 1024], P(None, 'tp'), may hold values from -3 to 3
- w_key: bfloat16 [1024, 512], P(None, 'tp'), may hold values from -2 to 2
- w_value: bfloat16 [1024, 512], P(None, 'tp'), may hold values from -0.1875 to 0.1875
- w_out: bfloat16 [1024, 1024], P('tp'), may hold values from -0.1875 to 0.1875
- norm2_gain: float32 [1024], replicated, may hold values from 0.25 to 1.75
- w_gate: bfloat16 [32, 1024, 512], P('seq'), may hold values from -0.1875 to 0.1875
- w_up: bfloat16 [32, 1024, 512], P('seq'), may hold values from -0.1875 to 0.1875
- w_down: bfloat16 [32, 512, 1024], P('seq'), may hold values from -0.25 to 0.25
- cache_in: bfloat16 [288, 256, 8, 128], P('seq', None, 'tp'), may hold values from -48 to 48
- cache_len: int32 [4], replicated, may hold values from 0 to 16384, as said below
- block_table: int32 [288], replicated, may hold values from 0 to 287, each once
- routes: int32 [8192, 8], P(('seq', 'tp')), may hold values from 0 to 31, all different within a row; in each aligned block of 32 rows (0 to 31, 32 to 63, ...) at most 12 rows name the same one
- gate_w: float32 [8192, 8], P(('seq', 'tp')), may hold values from 0.05 to 0.35
Outputs:
- hidden_out: bfloat16 [8192, 1024], P(('seq', 'tp'))
- cache_out: bfloat16 [288, 256, 8, 128], P('seq', None, 'tp')
Inputs may be any that keep to these rules, and one draw needn't show every extreme that they name: `cache_len`: some request holds exactly 16384 entries. `block_table`: each pool block appears once; pool block b lies on index b // 9 of seq. `routes`: each row names 8 different experts; among the rows of one device (aligned blocks of 32 rows) no expert is named more than 12 times, a bound that some block reaches.
All inputs are finite; a program needn't handle non-finite values.
Results may differ from a plain program's by a relative error of at most 0.035.
The roundings to bfloat16 on the way count: a program that leaves them out, or rounds other values in their place, can miss the bound.
Values may be sent and summed in bfloat16 or wider, within the bound.
No kernel may reach another device: no remote copies, remote signals or barrier semaphores. Data moves between devices by JAX's collectives and lax.ppermute only.
A program may use at most 128 MiB of HBM per device.

v0:
```python
import math
import jax
import jax.numpy as jnp
from jax import lax
from jax.sharding import PartitionSpec as P

D = 1024
HD = 64
GROUP = 2
TOP = 8
STRETCH = 2048
BS = 256
TOK_DEV = 256
MAXB = 72
norm_eps = 1e-05
rope_base = 10000.0
mask_fill = -1e30


def rms_scale(inputs, gains):
    floats = inputs.astype(jnp.float32)
    mean_square = jnp.mean(floats * floats, axis=-1, keepdims=True)
    return (floats * lax.rsqrt(mean_square + norm_eps) * gains).astype(jnp.bfloat16)


def rotate(vectors, positions):
    halfway = vectors.shape[-1] // 2
    counter = jnp.arange(halfway, dtype=jnp.int32).astype(jnp.float32)
    frequency = jnp.exp(counter * (-2.0 * math.log(rope_base) / vectors.shape[-1]))
    angles = positions.astype(jnp.float32)[:, None] * frequency[None, :]
    cosine = jnp.cos(angles)[:, None, :]
    sine_part = jnp.sin(angles)[:, None, :]
    front_half = vectors[..., :halfway]
    back_half = vectors[..., halfway:]
    return jnp.concatenate(
        [front_half * cosine - back_half * sine_part, back_half * cosine + front_half * sine_part],
        axis=-1,
    )


def on_device(
    hidden,
    norm1_gain,
    w_query,
    w_key,
    w_value,
    w_out,
    norm2_gain,
    w_gate,
    w_up,
    w_down,
    cache_in,
    cache_len,
    block_table,
    routes,
    gate_w,
):
    seq_count = lax.axis_size("seq")
    seq_place = lax.axis_index("seq")
    tp_place = lax.axis_index("tp")
    scaling = 1.0 / math.sqrt(HD)
    token_ids = seq_place * TOK_DEV + jnp.arange(TOK_DEV, dtype=jnp.int32)
    offsets = token_ids % STRETCH
    positions = cache_len[token_ids // STRETCH] + offsets
    normed = rms_scale(hidden, norm1_gain)
    queries = jnp.dot(normed, w_query, preferred_element_type=jnp.float32).reshape(
        TOK_DEV, GROUP, HD
    )
    queries = rotate(queries, positions).astype(jnp.bfloat16)
    key_rows = jnp.dot(normed, w_key, preferred_element_type=jnp.float32).reshape(TOK_DEV, 1, HD)
    key_rows = rotate(key_rows, positions).reshape(TOK_DEV, HD).astype(jnp.bfloat16)
    value_rows = jnp.dot(normed, w_value, preferred_element_type=jnp.float32).astype(jnp.bfloat16)
    new_rows = jnp.concatenate([key_rows, value_rows], axis=1)
    flat_queries = queries.reshape(TOK_DEV, GROUP * HD)
    all_queries, all_rows = (
        lax.all_gather(flat_queries, "seq", axis=0, tiled=True),
        lax.all_gather(new_rows, "seq", axis=0, tiled=True),
    )
    query_total = all_queries.shape[0]
    blk_count = cache_in.shape[0]
    pool_size = block_table.shape[0]
    pool_ids = seq_place * blk_count + jnp.arange(blk_count, dtype=jnp.int32)
    matched = block_table[None, :] == pool_ids[:, None]
    slot_of = jnp.sum(
        jnp.where(matched, jnp.arange(pool_size, dtype=jnp.int32)[None, :], 0), axis=1
    )
    block_req = slot_of // MAXB
    block_pos = slot_of % MAXB * BS
    cache_layer = cache_in[:, :, 0, :]
    span_rows = STRETCH * GROUP

    def update(block_id, states):
        row_peak, row_mass, row_accum = states
        request = block_req[block_id]
        first_row = request * span_rows
        filled = cache_len[request]
        entries = cache_layer[block_id]
        span_queries = lax.dynamic_slice_in_dim(all_queries, request * STRETCH, STRETCH, 0).reshape(
            span_rows, HD
        )
        scores = (
            jnp.einsum(
                "qd,kd->qk", span_queries, entries[:, :HD], preferred_element_type=jnp.float32
            )
            * scaling
        )
        visible = block_pos[block_id] + jnp.arange(BS, dtype=jnp.int32) < filled
        scores = jnp.where(visible[None, :], scores, mask_fill)
        old_peak = lax.dynamic_slice_in_dim(row_peak, first_row, span_rows, 0)
        new_peak = jnp.maximum(old_peak, jnp.max(scores, axis=-1))
        weights = jnp.where(visible[None, :], jnp.exp(scores - new_peak[:, None]), 0.0)
        retain = jnp.exp(old_peak - new_peak)
        old_mass = lax.dynamic_slice_in_dim(row_mass, first_row, span_rows, 0)
        old_accum = lax.dynamic_slice_in_dim(row_accum, first_row, span_rows, 0)
        mixed = jnp.einsum(
            "qk,kd->qd",
            weights.astype(jnp.bfloat16),
            entries[:, HD:],
            preferred_element_type=jnp.float32,
        )
        row_peak = lax.dynamic_update_slice_in_dim(row_peak, new_peak, first_row, 0)
        row_mass = lax.dynamic_update_slice_in_dim(
            row_mass, old_mass * retain + jnp.sum(weights, axis=-1), first_row, 0
        )
        row_accum = lax.dynamic_update_slice_in_dim(
            row_accum, old_accum * retain[:, None] + mixed, first_row, 0
        )
        return (row_peak, row_mass, row_accum)

    def visit_block(block_id, states):
        return update(block_id, states)

    flat_total = query_total * GROUP
    start_states = (
        jnp.full((flat_total,), mask_fill, jnp.float32),
        jnp.zeros((flat_total,), jnp.float32),
        jnp.zeros((flat_total, HD), jnp.float32),
    )
    row_peak, row_mass, row_accum = lax.fori_loop(0, blk_count, visit_block, start_states)
    each_peak, each_mass, each_accum = (
        lax.all_to_all(
            row_peak.reshape(seq_count, TOK_DEV * GROUP),
            "seq",
            split_axis=0,
            concat_axis=0,
            tiled=True,
        ),
        lax.all_to_all(
            row_mass.reshape(seq_count, TOK_DEV * GROUP),
            "seq",
            split_axis=0,
            concat_axis=0,
            tiled=True,
        ),
        lax.all_to_all(
            row_accum.reshape(seq_count, TOK_DEV, GROUP * HD),
            "seq",
            split_axis=0,
            concat_axis=0,
            tiled=True,
        ),
    )
    top_peak = jnp.max(each_peak, axis=0)
    factor = jnp.exp(each_peak - top_peak[None])
    got_mass = jnp.sum(each_mass * factor, axis=0).reshape(TOK_DEV, GROUP)
    got_accum = jnp.sum(
        each_accum.reshape(seq_count, TOK_DEV * GROUP, HD) * factor[..., None], axis=0
    ).reshape(TOK_DEV, GROUP, HD)
    my_peak = top_peak.reshape(TOK_DEV, GROUP)
    own_request = seq_place * TOK_DEV // STRETCH
    own_rows = lax.dynamic_slice_in_dim(all_rows, own_request * STRETCH, STRETCH, 0)
    own_queries = queries.reshape(TOK_DEV * GROUP, HD)
    self_scores = (
        jnp.einsum("qd,kd->qk", own_queries, own_rows[:, :HD], preferred_element_type=jnp.float32)
        * scaling
    )
    row_offsets = jnp.repeat(offsets, GROUP)
    causal = jnp.arange(STRETCH, dtype=jnp.int32)[None, :] <= row_offsets[:, None]
    self_scores = jnp.where(causal, self_scores, mask_fill)
    self_peak = jnp.max(self_scores, axis=-1)
    self_weights = jnp.where(causal, jnp.exp(self_scores - self_peak[:, None]), 0.0)
    self_mass = jnp.sum(self_weights, axis=-1).reshape(TOK_DEV, GROUP)
    self_accum = jnp.einsum(
        "qk,kd->qd",
        self_weights.astype(jnp.bfloat16),
        own_rows[:, HD:],
        preferred_element_type=jnp.float32,
    ).reshape(TOK_DEV, GROUP, HD)
    self_peak = self_peak.reshape(TOK_DEV, GROUP)
    final_peak = jnp.maximum(my_peak, self_peak)
    cache_share = jnp.exp(my_peak - final_peak)
    self_share = jnp.exp(self_peak - final_peak)
    denom = got_mass * cache_share + self_mass * self_share
    attention = (got_accum * cache_share[..., None] + self_accum * self_share[..., None]) / denom[
        ..., None
    ]
    attention = attention.reshape(TOK_DEV, GROUP * HD).astype(jnp.bfloat16)
    tp_rows = TOK_DEV // lax.axis_size("tp")
    head_total = lax.psum_scatter(
        jnp.dot(attention, w_out, preferred_element_type=jnp.float32).astype(jnp.bfloat16),
        "tp",
        scatter_dimension=0,
        tiled=True,
    ).astype(jnp.float32)
    own_hidden = lax.dynamic_slice_in_dim(hidden, tp_place * tp_rows, tp_rows, 0)
    residual = (own_hidden.astype(jnp.float32) + head_total).astype(jnp.bfloat16)
    normed2 = rms_scale(residual, norm2_gain)
    capacity = min(tp_rows, 3 * tp_rows * TOP // (2 * seq_count))
    flat_expert = routes.reshape(tp_rows * TOP)
    onehot = (flat_expert[:, None] == jnp.arange(seq_count, dtype=jnp.int32)[None, :]).astype(
        jnp.int32
    )
    ranking = jnp.sum((jnp.cumsum(onehot, axis=0) - onehot) * onehot, axis=1)
    slot_ids = flat_expert * capacity + ranking
    sources = jnp.arange(tp_rows * TOP, dtype=jnp.int32) // TOP
    table = jnp.zeros((seq_count * capacity,), jnp.int32).at[slot_ids].set(sources)
    occupied = jnp.zeros((seq_count * capacity,), jnp.bool_).at[slot_ids].set(True)
    outgoing = jnp.where(occupied[:, None], normed2[table], jnp.zeros((), jnp.bfloat16)).reshape(
        seq_count, capacity, D
    )
    incoming = lax.all_to_all(outgoing, "seq", split_axis=0, concat_axis=0, tiled=True)
    senders = incoming.shape[0]
    items = incoming.shape[1]
    flat_rows = incoming.reshape(senders * items, D)
    gate_part = jnp.dot(flat_rows, w_gate[0], preferred_element_type=jnp.float32)
    up_part = jnp.dot(flat_rows, w_up[0], preferred_element_type=jnp.float32)
    inner = (jax.nn.silu(gate_part) * up_part).astype(jnp.bfloat16)
    answer = jnp.dot(inner, w_down[0], preferred_element_type=jnp.float32).astype(jnp.bfloat16)
    answered = answer.reshape(senders, items, D)
    returned = lax.all_to_all(answered, "seq", split_axis=0, concat_axis=0, tiled=True)
    picked = returned.reshape(seq_count * capacity, D)[slot_ids].reshape(tp_rows, TOP, D)
    expert_sum = jnp.sum(gate_w[..., None] * picked.astype(jnp.float32), axis=1)
    hidden_out = (residual.astype(jnp.float32) + expert_sum).astype(jnp.bfloat16)
    block_offsets = block_pos[:, None] + jnp.arange(BS, dtype=jnp.int32)[None, :]
    block_fill = cache_len[block_req][:, None]
    inside = (block_offsets >= block_fill) & (block_offsets < block_fill + STRETCH)
    source_rows = block_req[:, None] * STRETCH + jnp.clip(
        block_offsets - block_fill, 0, STRETCH - 1
    )
    fresh = all_rows[source_rows]
    cache_out = jnp.where(inside[..., None], fresh, cache_layer)[:, :, None, :]
    return (hidden_out, cache_out)


def solution(mesh):
    placed = (
        P("seq", None),
        P(),
        P(None, "tp"),
        P(None, "tp"),
        P(None, "tp"),
        P("tp", None),
        P(),
        P("seq", None, None),
        P("seq", None, None),
        P("seq", None, None),
        P("seq", None, "tp", None),
        P(),
        P(),
        P(("seq", "tp"), None),
        P(("seq", "tp"), None),
    )
    return jax.shard_map(
        on_device,
        mesh=mesh,
        in_specs=placed,
        out_specs=(P(("seq", "tp"), None), P("seq", None, "tp", None)),
        check_vma=False,
    )
```

profile of v0, /device:TPU:1, one launch (start us, length us, event | category | flops | bytes accessed | tf_op | source)
XLA Modules:
  0.0 443.7 jit_solution(978709974458189872)
XLA Ops:
  19.0 49.9 %all-gather.3.cloned.1.call-done = bf16[8192,128]{0,1:T(8,128)(2,1)} async-done(((bf16[256,128]{0,1:T(8,128)(2,1)}), bf16[8192,128]{0,1:T(8,128)(2,1)}) %all-gather.3.cloned.1.call-update) | async-done | bytes 2097168 | tf_op jit(solution)/shard_map/all_gather | solution.py:76
  71.8 170.7 %while.17 = (s32[]{:T(128)}, f32[16384]{0:T(1024)S(1)}, f32[16384]{0:T(1024)}, f32[16384,64]{0,1:T(8,128)}, s32[9]{0:T(128)S(1)}, /*index=5*/s32[9]{0:T(128)S(1)...) while((s32[]{:T(128)}, f32[16384]{0:T(1024)S(1)}, ...), condition=%wide.region_5.6_spmd, body=%wide.region_2.5_spmd.sunk | while | flops 278405632 | bytes 35898736 | solution.py:139
  83.2 3.2 fusion.103
  144.6 3.1 fusion.104
  163.6 3.1 fusion.104
  242.6 12.3 %all_to_all.39 = f32[32,1,512]{2,1,0:T(1,128)S(1)} all-to-all(f32[32,1,512]{2,1,0:T(1,128)S(1)} %bitcast.101), channel_id=1, replica_groups=mesh['seq'=32,'tp'=8] {'seq'}, dimensions={0} | all-to-all | bytes 131072 | tf_op jit(solution)/shard_map/all_to_all | solution.py:141
  254.9 3.9 all-to-all-start.2
  258.8 6.9 %copy.74 = f32[16384,64]{1,0:T(8,128)} copy(f32[16384,64]{0,1:T(8,128)} %get-tuple-element.158) | data formatting | bytes 8388608 | tf_op jit(solution)/shard_map/while | solution.py:139
  265.7 7.2 %reshape.606 = f32[32,256,128]{2,1,0:T(8,128)} reshape(f32[16384,64]{1,0:T(8,128)} %copy.74) | data formatting | bytes 8388608 | tf_op jit(solution)/shard_map/reshape | solution.py:156
  272.9 7.7 %all-to-all-start = ((f32[32,256,128]{2,1,0:T(8,128)}), f32[32,256,128]{2,1,0:T(8,128)}, u32[]{:S(2)}, u32[]{:S(2)}) async-start(f32[32,256,128]{2,1,0:T(8,128)} %reshape.606), calls=%async_computation | async-start | bytes 8388608 | tf_op jit(solution)/shard_map/all_to_all | solution.py:155
  282.2 3.8 fusion.11
  286.1 3.5 fusion.12
  289.9 3.4 fusion.14
  293.7 4.5 %mul.312 = f32[32,512,64]{2,1,0:T(8,128)} broadcast(f32[32,512]{1,0:T(8,128)S(1)} %get-tuple-element.228), dimensions={0,1} | broadcast | bytes 4259840 | tf_op jit(solution)/shard_map/mul | solution.py:167
  298.3 7.2 %mul.313 = f32[32,256,128]{2,1,0:T(8,128)} reshape(f32[32,512,64]{2,1,0:T(8,128)} %mul.312) | data formatting | bytes 8388608 | tf_op jit(solution)/shard_map/mul | solution.py:167
  306.2 26.5 %all-to-all-done = f32[32,256,128]{2,1,0:T(8,128)} async-done(((f32[32,256,128]{2,1,0:T(8,128)}), f32[32,256,128]{2,1,0:T(8,128)}, u32[]{:S(2)}, u32[]{:S(2)}) %all-to-all-start) | async-done | bytes 4194336 | tf_op jit(solution)/shard_map/all_to_all | solution.py:155
  332.7 3.9 multiply_reduce_fusion
  341.4 30.2 %reduce-scatter.2.cloned.1.call-done = bf16[32,1024]{1,0:T(8,128)(2,1)} async-done(((bf16[256,1024]{1,0:T(8,128)(2,1)}), bf16[32,1024]{1,0:T(8,128)(2,1)}) %reduce-scatter.2.cloned.1.call-update) | async-done | bytes 65552 | tf_op jit(solution)/shard_map/reduce_scatter | solution.py:199
  376.1 12.3 %all-to-all-start.3 = ((bf16[32,12,1024]{2,1,0:T(8,128)(2,1)}), bf16[32,12,1024]{2,1,0:T(8,128)(2,1)S(1)}, u32[]{:S(2)}, u32[]{:S(2)}) async-start(bf16[32,12,1024]{2,1,0:T(8,128)(2,1)} %broadcast_select_fusion), calls=%async_computation.4 | async-start | bytes 2097152 | tf_op jit(solution)/shard_map/all_to_all | solution.py:221
  389.2 16.1 %all-to-all-done.3 = bf16[32,12,1024]{2,1,0:T(8,128)(2,1)S(1)} async-done(((bf16[32,12,1024]{2,1,0:T(8,128)(2,1)}), bf16[32,12,1024]{2,1,0:T(8,128)(2,1)S(1)}, u32[]{:S(2)}, u32[]{:S(2)}) %all-to-all-start.3) | async-done | bytes 786464 | tf_op jit(solution)/shard_map/all_to_all | solution.py:221
  412.0 4.7 %all-to-all-start.4 = ((bf16[32,12,1024]{2,1,0:T(8,128)(2,1)}), bf16[32,12,1024]{2,1,0:T(8,128)(2,1)}, u32[]{:S(2)}, u32[]{:S(2)}) async-start(bf16[32,12,1024]{2,1,0:T(8,128)(2,1)} %reshape.615), calls=%async_computation.5 | async-start | bytes 2097152 | tf_op jit(solution)/shard_map/all_to_all | solution.py:230
  416.9 3.2 copy.92
  420.1 5.6 %gather_fusion.3 = bf16[2304,128]{1,0:T(8,128)(2,1)} fusion(bf16[8192,128]{1,0:T(8,128)(2,1)S(1)} %copy.92, s32[3072]{0:T(1024)S(1)} %pad_clamp_fusion), kind=kCustom, calls=%fused_computation.3 | custom fusion | bytes 1188864 | tf_op jit(solution)/shard_map/gather | solution.py:240
  427.9 5.7 %all-to-all-done.4 = bf16[32,12,1024]{2,1,0:T(8,128)(2,1)} async-done(((bf16[32,12,1024]{2,1,0:T(8,128)(2,1)}), bf16[32,12,1024]{2,1,0:T(8,128)(2,1)}, u32[]{:S(2)}, u32[]{:S(2)}) %all-to-all-start.4) | async-done | bytes 786464 | tf_op jit(solution)/shard_map/all_to_all | solution.py:230
  (261 shorter events, 174.8 us)
Async XLA Ops:
  7.2 401.0 %copy-start = (bf16[1,512,1024]{2,1,0:T(8,128)(2,1)S(1)}, bf16[1,512,1024]{2,1,0:T(8,128)(2,1)}, u32[]{:S(2)}) copy-start(bf16[1,512,1024]{2,1,0:T(8,128)(2,1)} %param.26) | copy-start | bytes 3145732
  7.2 11.6 %copy-start.7 = (s32[288]{0:T(512)S(1)}, s32[288]{0:T(512)}, u32[]{:S(2)}) copy-start(s32[288]{0:T(512)} %param.29) | copy-start | bytes 3460
  7.2 61.7 %all-gather.3.cloned.1.call-start = ((), (), s32[]{:S(2)}) async-start(), calls=%async_computation.6 | async-start | bytes 2162688 | tf_op jit(solution)/shard_map/all_gather | solution.py:76
  12.8 59.1 %copy-start.2 = (s32[4]{0:T(128)S(1)}, s32[4]{0:T(128)}, u32[]{:S(2)}) copy-start(s32[4]{0:T(128)} %param.28) | copy-start | bytes 52
  15.0 267.2 %all-gather.5.cloned.1.call-start = ((), (), s32[]{:S(2)}) async-start(), calls=%async_computation.7 | async-start | bytes 2162688 | tf_op jit(solution)/shard_map/all_gather | solution.py:77
  83.1 4.6 %copy-start.1 = (f32[4096,256]{0,1:T(8,128)S(1)}, f32[4096,256]{0,1:T(8,128)}, u32[]{:S(2)}) copy-start(f32[4096,256]{0,1:T(8,128)} %get-tuple-element.309) | copy-start | bytes 12582916 | tf_op jit(solution)/shard_map/while
  102.1 4.5 %copy-start.1 = (f32[4096,256]{0,1:T(8,128)S(1)}, f32[4096,256]{0,1:T(8,128)}, u32[]{:S(2)}) copy-start(f32[4096,256]{0,1:T(8,128)} %get-tuple-element.309) | copy-start | bytes 12582916 | tf_op jit(solution)/shard_map/while
  121.1 4.5 %copy-start.1 = (f32[4096,256]{0,1:T(8,128)S(1)}, f32[4096,256]{0,1:T(8,128)}, u32[]{:S(2)}) copy-start(f32[4096,256]{0,1:T(8,128)} %get-tuple-element.309) | copy-start | bytes 12582916 | tf_op jit(solution)/shard_map/while
  140.1 4.5 %copy-start.1 = (f32[4096,256]{0,1:T(8,128)S(1)}, f32[4096,256]{0,1:T(8,128)}, u32[]{:S(2)}) copy-start(f32[4096,256]{0,1:T(8,128)} %get-tuple-element.309) | copy-start | bytes 12582916 | tf_op jit(solution)/shard_map/while
  159.1 4.5 %copy-start.1 = (f32[4096,256]{0,1:T(8,128)S(1)}, f32[4096,256]{0,1:T(8,128)}, u32[]{:S(2)}) copy-start(f32[4096,256]{0,1:T(8,128)} %get-tuple-element.309) | copy-start | bytes 12582916 | tf_op jit(solution)/shard_map/while
  178.1 4.5 %copy-start.1 = (f32[4096,256]{0,1:T(8,128)S(1)}, f32[4096,256]{0,1:T(8,128)}, u32[]{:S(2)}) copy-start(f32[4096,256]{0,1:T(8,128)} %get-tuple-element.309) | copy-start | bytes 12582916 | tf_op jit(solution)/shard_map/while
  197.0 4.5 %copy-start.1 = (f32[4096,256]{0,1:T(8,128)S(1)}, f32[4096,256]{0,1:T(8,128)}, u32[]{:S(2)}) copy-start(f32[4096,256]{0,1:T(8,128)} %get-tuple-element.309) | copy-start | bytes 12582916 | tf_op jit(solution)/shard_map/while
  216.0 4.5 %copy-start.1 = (f32[4096,256]{0,1:T(8,128)S(1)}, f32[4096,256]{0,1:T(8,128)}, u32[]{:S(2)}) copy-start(f32[4096,256]{0,1:T(8,128)} %get-tuple-element.309) | copy-start | bytes 12582916 | tf_op jit(solution)/shard_map/while
  234.9 4.5 %copy-start.1 = (f32[4096,256]{0,1:T(8,128)S(1)}, f32[4096,256]{0,1:T(8,128)}, u32[]{:S(2)}) copy-start(f32[4096,256]{0,1:T(8,128)} %get-tuple-element.309) | copy-start | bytes 12582916 | tf_op jit(solution)/shard_map/while
  254.9 18.0 %all-to-all-start.2 = ((f32[32,1,512]{2,1,0:T(1,128)}), f32[32,1,512]{2,1,0:T(1,128)S(1)}, u32[]{:S(2)}, u32[]{:S(2)}) async-start(f32[32,1,512]{2,1,0:T(1,128)} %bitcast.19), calls=%async_computation.2 | async-start | bytes 131072 | tf_op jit(solution)/shard_map/all_to_all | solution.py:148
  272.9 8.4 %copy-start.4 = (s32[32,8]{0,1:T(8,128)S(1)}, s32[32,8]{0,1:T(8,128)}, u32[]{:S(2)}) copy-start(s32[32,8]{0,1:T(8,128)} %param.30) | copy-start | bytes 3076
  272.9 59.8 %all-to-all-start = ((f32[32,256,128]{2,1,0:T(8,128)}), f32[32,256,128]{2,1,0:T(8,128)}, u32[]{:S(2)}, u32[]{:S(2)}) async-start(f32[32,256,128]{2,1,0:T(8,128)} %reshape.606), calls=%async_computation | async-start | bytes 8388608 | tf_op jit(solution)/shard_map/all_to_all | solution.py:155
  280.6 91.0 %reduce-scatter.2.cloned.1.call-start = ((), (), s32[]{:S(2)}) async-start(), calls=%async_computation.8 | async-start | bytes 589824 | tf_op jit(solution)/shard_map/reduce_scatter | solution.py:199
  306.2 30.4 %copy-start.3 = (bf16[128,1024]{1,0:T(8,128)(2,1)S(1)}, bf16[128,1024]{1,0:T(8,128)(2,1)}, u32[]{:S(2)}) copy-start(bf16[128,1024]{1,0:T(8,128)(2,1)} %param.22) | copy-start | bytes 786436
  306.2 66.4 %copy-start.5 = (f32[1024]{0:T(1024)S(1)}, f32[1024]{0:T(1024)}, u32[]{:S(2)}) copy-start(f32[1024]{0:T(1024)} %param.23) | copy-start | bytes 12292
  376.1 29.2 %all-to-all-start.3 = ((bf16[32,12,1024]{2,1,0:T(8,128)(2,1)}), bf16[32,12,1024]{2,1,0:T(8,128)(2,1)S(1)}, u32[]{:S(2)}, u32[]{:S(2)}) async-start(bf16[32,12,1024]{2,1,0:T(8,128)(2,1)} %broadcast_select_fusion), calls=%async_computation.4 | async-start | bytes 2097152 | tf_op jit(solution)/shard_map/all_to_all | solution.py:221
  408.2 8.5 %copy-start.6 = (f32[32,8]{0,1:T(8,128)S(1)}, f32[32,8]{0,1:T(8,128)}, u32[]{:S(2)}) copy-start(f32[32,8]{0,1:T(8,128)} %param.31) | copy-start | bytes 3076
  412.0 21.6 %all-to-all-start.4 = ((bf16[32,12,1024]{2,1,0:T(8,128)(2,1)}), bf16[32,12,1024]{2,1,0:T(8,128)(2,1)}, u32[]{:S(2)}, u32[]{:S(2)}) async-start(bf16[32,12,1024]{2,1,0:T(8,128)(2,1)} %reshape.615), calls=%async_computation.5 | async-start | bytes 2097152 | tf_op jit(solution)/shard_map/all_to_all | solution.py:230
Sparse Core Ops, SparseCore 0:
  15.1 53.7 all-gather.2
  71.9 49.0 all-gather.4
  337.8 33.6 reduce-scatter.1
where the time goes:
time: 447 us; the launch traced here: 444 us
  waiting for transfers between devices  128 us (29%)
  local copies, waits for them, and re-layouts  91.9 us (21%)
  other arithmetic  71.6 us (16%)
  matrix products  69.7 us (16%)
  starting transfers between devices  28.9 us (6%)
  loops' own time  26.6 us (6%)
  between operations  14.3 us (3%)
  blocking collectives  12.3 us (3%)
    all_gather x1, waiting for transfers between devices, on_device(): lax.all_gather(flat_queries, 'seq', axis=0, tiled=True)  49.9 us
    reduce_scatter x1, waiting for transfers between devices, on_device(): lax.psum_scatter(jnp.dot(attention, w_out, preferred_element_type=jnp.flo...  30.2 us
    reduce_sum x9, other arithmetic, update(): jnp.sum(weights, axis=-1)  28.2 us
    dot_general x9, matrix products, update(): jnp.einsum('qk,kd->qd', weights.astype(jnp.bfloat16), entries[:, HD:], pr...  28.1 us
    another operation x1, loops' own time, on_device(): lax.fori_loop(0, blk_count, visit_block, start_states)  26.6 us
    all_to_all x1, waiting for transfers between devices, on_device(): lax.all_to_all(row_accum.reshape(seq_count, TOK_DEV, GROUP * HD), 'seq',...  26.5 us
    dot_general x9, matrix products, update(): jnp.einsum('qd,kd->qk', span_queries, entries[:, :HD], preferred_element_...  23.7 us
    all_to_all x1, waiting for transfers between devices, on_device(): lax.all_to_all(outgoing, 'seq', split_axis=0, concat_axis=0, tiled=True)  16.1 us
  transfers between devices with their start and end apart: 7, of which 5 were waited for; matrix products, arithmetic and copies ran while one was open for 46% of the time, Pallas kernels for 0%

commit v1 on v0

--- a/solution.py
+++ b/solution.py
@@ -72,8 +72,15 @@
     value_rows = jnp.dot(normed, w_value, preferred_element_type=jnp.float32).astype(jnp.bfloat16)
     new_rows = jnp.concatenate([key_rows, value_rows], axis=1)
     flat_queries = queries.reshape(TOK_DEV, GROUP * HD)
+
+    def streams_see(x_in, mesh_ax, array_dim):
+        step_out = jnp.stack([x_in for _ in range(lax.axis_size(mesh_ax))])
+        earlier = lax.all_to_all(step_out, mesh_ax, 0, 0)
+        then = jnp.concatenate(earlier, axis=array_dim)
+        return then
+
     all_queries, all_rows = (
-        lax.all_gather(flat_queries, "seq", axis=0, tiled=True),
+        streams_see(flat_queries, "seq", 0),
         lax.all_gather(new_rows, "seq", axis=0, tiled=True),
     )
     query_total = all_queries.shape[0]

time: 447 us -> 430 us (0.962)
  waiting for transfers between devices: 128 us -> 107 us
  starting transfers between devices: 28.9 us -> 37.4 us
    all_gather x1 -> x0, waiting for transfers between devices: 49.9 us -> none  [on_device(): lax.all_gather(flat_queries, 'seq', axis=0, tiled=True)]
    all_to_all x0 -> x1, waiting for transfers between devices: none -> 26.5 us  [streams_see(): earlier = lax.all_to_all(step_out, mesh_ax, 0, 0)]
    all_to_all x0 -> x1, starting transfers between devices: none -> 8.63 us  [streams_see(): earlier = lax.all_to_all(step_out, mesh_ax, 0, 0)]
    dynamic_slice x18 -> x9, local copies, waits for them, and re-layouts: 12.4 us -> 9.73 us  [update(): lax.dynamic_slice_in_dim(all_queries, request * STRETCH, STRETCH, 0)]
  transfers between devices with their start and end apart: 7 -> 7, of which waited for: 5 -> 5; matrix products, arithmetic and copies ran while one was open for 46% -> 47% of each run, Pallas kernels for 0% -> 0%
where the time goes in v1:
time: 430 us; the launch traced here: 426 us
  waiting for transfers between devices  107 us (25%)
  local copies, waits for them, and re-layouts  91.2 us (21%)
  other arithmetic  70.9 us (16%)
  matrix products  67.5 us (16%)
  starting transfers between devices  37.4 us (9%)
  loops' own time  26.5 us (6%)
  between operations  14.6 us (3%)
  blocking collectives  11.6 us (3%)
    reduce_scatter x1, waiting for transfers between devices, on_device(): lax.psum_scatter(jnp.dot(attention, w_out, preferred_element_type=jnp.flo...  31.8 us
    reduce_sum x9, other arithmetic, update(): jnp.sum(weights, axis=-1)  28.2 us
    dot_general x9, matrix products, update(): jnp.einsum('qk,kd->qd', weights.astype(jnp.bfloat16), entries[:, HD:], pr...  28 us
    all_to_all x1, waiting for transfers between devices, streams_see(): earlier = lax.all_to_all(step_out, mesh_ax, 0, 0)  26.5 us
    all_to_all x1, waiting for transfers between devices, on_device(): lax.all_to_all(row_accum.reshape(seq_count, TOK_DEV, GROUP * HD), 'seq',...  26.5 us
    another operation x1, loops' own time, on_device(): lax.fori_loop(0, blk_count, visit_block, start_states)  26.5 us
    dot_general x9, matrix products, update(): jnp.einsum('qd,kd->qk', span_queries, entries[:, :HD], preferred_element_...  23.7 us
    all_to_all x1, waiting for transfers between devices, on_device(): lax.all_to_all(outgoing, 'seq', split_axis=0, concat_axis=0, tiled=True)  16.1 us
  transfers between devices with their start and end apart: 7, of which 5 were waited for; matrix products, arithmetic and copies ran while one was open for 47% of the time, Pallas kernels for 0%

profile of v1, /device:TPU:1, one launch (start us, length us, event | category | flops | bytes accessed | tf_op | source)
XLA Modules:
  0.0 426.5 jit_solution(17631041410842052886)
XLA Ops:
  16.3 8.6 %all-to-all-start = ((bf16[32,256,128]{2,1,0:T(8,128)(2,1)}), bf16[32,256,128]{2,1,0:T(8,128)(2,1)}, u32[]{:S(2)}, u32[]{:S(2)}) async-start(bf16[32,256,128]{2,1,0:T(8,128)(2,1)} %stack.3), calls=%async_computation | async-start | bytes 4194304 | tf_op jit(solution)/shard_map/all_to_all | solution.py:78
  26.9 26.5 %all-to-all-done = bf16[32,256,128]{2,1,0:T(8,128)(2,1)} async-done(((bf16[32,256,128]{2,1,0:T(8,128)(2,1)}), bf16[32,256,128]{2,1,0:T(8,128)(2,1)}, u32[]{:S(2)}, u32[]{:S(2)}) %all-to-all-start) | async-done | bytes 2097184 | tf_op jit(solution)/shard_map/all_to_all | solution.py:78
  56.3 167.9 %while.17 = (s32[]{:T(128)}, f32[16384]{0:T(1024)S(1)}, f32[16384]{0:T(1024)}, f32[16384,64]{0,1:T(8,128)}, s32[9]{0:T(128)S(1)}, /*index=5*/s32[9]{0:T(128)S(1)...) while((s32[]{:T(128)}, f32[16384]{0:T(1024)S(1)}, ...), condition=%wide.region_5.6_spmd, body=%wide.region_2.5_spmd.sunk | while | flops 278405632 | bytes 34850160 | solution.py:146
  127.8 3.1 fusion.104
  221.1 3.1 fusion.104
  224.3 11.6 %all_to_all.44 = f32[32,1,512]{2,1,0:T(1,128)S(1)} all-to-all(f32[32,1,512]{2,1,0:T(1,128)S(1)} %bitcast.102), channel_id=1, replica_groups=mesh['seq'=32,'tp'=8] {'seq'}, dimensions={0} | all-to-all | bytes 131072 | tf_op jit(solution)/shard_map/all_to_all | solution.py:148
  235.8 3.9 all-to-all-start.3
  239.7 6.9 %copy.89 = f32[16384,64]{1,0:T(8,128)} copy(f32[16384,64]{0,1:T(8,128)} %get-tuple-element.158) | data formatting | bytes 8388608 | tf_op jit(solution)/shard_map/while | solution.py:146
  246.6 7.2 %reshape.611 = f32[32,256,128]{2,1,0:T(8,128)} reshape(f32[16384,64]{1,0:T(8,128)} %copy.89) | data formatting | bytes 8388608 | tf_op jit(solution)/shard_map/reshape | solution.py:163
  253.9 7.7 %all-to-all-start.1 = ((f32[32,256,128]{2,1,0:T(8,128)}), f32[32,256,128]{2,1,0:T(8,128)}, u32[]{:S(2)}, u32[]{:S(2)}) async-start(f32[32,256,128]{2,1,0:T(8,128)} %reshape.611), calls=%async_computation.1 | async-start | bytes 8388608 | tf_op jit(solution)/shard_map/all_to_all | solution.py:162
  263.4 4.5 %mul.312 = f32[32,512,64]{2,1,0:T(8,128)} broadcast(f32[32,512]{1,0:T(8,128)S(1)} %get-tuple-element.192), dimensions={0,1} | broadcast | bytes 4259840 | tf_op jit(solution)/shard_map/mul | solution.py:174
  267.9 7.2 %mul.313 = f32[32,256,128]{2,1,0:T(8,128)} reshape(f32[32,512,64]{2,1,0:T(8,128)} %mul.312) | data formatting | bytes 8388608 | tf_op jit(solution)/shard_map/mul | solution.py:174
  275.5 3.8 fusion.11
  279.4 3.5 fusion.12
  283.6 3.4 fusion.14
  287.2 26.5 %all-to-all-done.1 = f32[32,256,128]{2,1,0:T(8,128)} async-done(((f32[32,256,128]{2,1,0:T(8,128)}), f32[32,256,128]{2,1,0:T(8,128)}, u32[]{:S(2)}, u32[]{:S(2)}) %all-to-all-start.1) | async-done | bytes 4194336 | tf_op jit(solution)/shard_map/all_to_all | solution.py:162
  313.7 3.9 multiply_reduce_fusion
  322.3 31.8 %reduce-scatter.2.cloned.1.call-done = bf16[32,1024]{1,0:T(8,128)(2,1)} async-done(((bf16[256,1024]{1,0:T(8,128)(2,1)}), bf16[32,1024]{1,0:T(8,128)(2,1)}) %reduce-scatter.2.cloned.1.call-update) | async-done | bytes 65552 | tf_op jit(solution)/shard_map/reduce_scatter | solution.py:206
  358.6 12.3 %all-to-all-start.4 = ((bf16[32,12,1024]{2,1,0:T(8,128)(2,1)}), bf16[32,12,1024]{2,1,0:T(8,128)(2,1)S(1)}, u32[]{:S(2)}, u32[]{:S(2)}) async-start(bf16[32,12,1024]{2,1,0:T(8,128)(2,1)} %broadcast_select_fusion), calls=%async_computation.5 | async-start | bytes 2097152 | tf_op jit(solution)/shard_map/all_to_all | solution.py:228
  371.7 16.1 %all-to-all-done.4 = bf16[32,12,1024]{2,1,0:T(8,128)(2,1)S(1)} async-done(((bf16[32,12,1024]{2,1,0:T(8,128)(2,1)}), bf16[32,12,1024]{2,1,0:T(8,128)(2,1)S(1)}, u32[]{:S(2)}, u32[]{:S(2)}) %all-to-all-start.4) | async-done | bytes 786464 | tf_op jit(solution)/shard_map/all_to_all | solution.py:228
  394.5 4.7 %all-to-all-start.5 = ((bf16[32,12,1024]{2,1,0:T(8,128)(2,1)}), bf16[32,12,1024]{2,1,0:T(8,128)(2,1)}, u32[]{:S(2)}, u32[]{:S(2)}) async-start(bf16[32,12,1024]{2,1,0:T(8,128)(2,1)} %reshape.620), calls=%async_computation.6 | async-start | bytes 2097152 | tf_op jit(solution)/shard_map/all_to_all | solution.py:237
  399.4 3.2 copy.107
  402.6 5.6 %gather_fusion.3 = bf16[2304,128]{1,0:T(8,128)(2,1)} fusion(bf16[8192,128]{1,0:T(8,128)(2,1)S(1)} %copy.107, s32[3072]{0:T(1024)S(1)} %pad_clamp_fusion), kind=kCustom, calls=%fused_computation.3 | custom fusion | bytes 1188864 | tf_op jit(solution)/shard_map/gather | solution.py:247
  410.4 5.7 %all-to-all-done.5 = bf16[32,12,1024]{2,1,0:T(8,128)(2,1)} async-done(((bf16[32,12,1024]{2,1,0:T(8,128)(2,1)}), bf16[32,12,1024]{2,1,0:T(8,128)(2,1)}, u32[]{:S(2)}, u32[]{:S(2)}) %all-to-all-start.5) | async-done | bytes 786464 | tf_op jit(solution)/shard_map/all_to_all | solution.py:237
  (261 shorter events, 174.3 us)
Async XLA Ops:
  7.2 383.5 %copy-start = (bf16[1,512,1024]{2,1,0:T(8,128)(2,1)S(1)}, bf16[1,512,1024]{2,1,0:T(8,128)(2,1)}, u32[]{:S(2)}) copy-start(bf16[1,512,1024]{2,1,0:T(8,128)(2,1)} %param.26) | copy-start | bytes 3145732
  11.3 13.8 %copy-start.3 = (bf16[256,1024]{1,0:T(8,128)(2,1)S(1)}, bf16[256,1024]{1,0:T(8,128)(2,1)}, u32[]{:S(2)}) copy-start(bf16[256,1024]{1,0:T(8,128)(2,1)} %param.17) | copy-start | bytes 1572868
  11.3 13.8 %copy-start.9 = (bf16[1024,64]{0,1:T(8,128)(2,1)S(1)}, bf16[1024,64]{0,1:T(8,128)(2,1)}, u32[]{:S(2)}) copy-start(bf16[1024,64]{0,1:T(8,128)(2,1)} %param.20) | copy-start | bytes 393220
  11.3 13.8 %copy-start.11 = (f32[1024]{0:T(1024)S(1)}, f32[1024]{0:T(1024)}, u32[]{:S(2)}) copy-start(f32[1024]{0:T(1024)} %param.18) | copy-start | bytes 12292
  14.3 11.3 %copy-start.10 = (bf16[1024,64]{0,1:T(8,128)(2,1)S(1)}, bf16[1024,64]{0,1:T(8,128)(2,1)}, u32[]{:S(2)}) copy-start(bf16[1024,64]{0,1:T(8,128)(2,1)} %param.21) | copy-start | bytes 393220
  14.5 12.2 %copy-start.8 = (s32[288]{0:T(512)S(1)}, s32[288]{0:T(512)}, u32[]{:S(2)}) copy-start(s32[288]{0:T(512)} %param.29) | copy-start | bytes 3460
  16.3 37.1 %all-to-all-start = ((bf16[32,256,128]{2,1,0:T(8,128)(2,1)}), bf16[32,256,128]{2,1,0:T(8,128)(2,1)}, u32[]{:S(2)}, u32[]{:S(2)}) async-start(bf16[32,256,128]{2,1,0:T(8,128)(2,1)} %stack.3), calls=%async_computation | async-start | bytes 4194304 | tf_op jit(solution)/shard_map/all_to_all | solution.py:78
  25.0 31.4 %copy-start.2 = (s32[4]{0:T(128)S(1)}, s32[4]{0:T(128)}, u32[]{:S(2)}) copy-start(s32[4]{0:T(128)} %param.28) | copy-start | bytes 52
  25.0 250.5 %all-gather.2.cloned.1.call-start = ((), (), s32[]{:S(2)}) async-start(), calls=%async_computation.7 | async-start | bytes 2162688 | tf_op jit(solution)/shard_map/all_gather | solution.py:84
  67.4 4.5 %copy-start.1 = (f32[4096,256]{0,1:T(8,128)S(1)}, f32[4096,256]{0,1:T(8,128)}, u32[]{:S(2)}) copy-start(f32[4096,256]{0,1:T(8,128)} %get-tuple-element.273) | copy-start | bytes 12582916 | tf_op jit(solution)/shard_map/while
  86.0 4.5 %copy-start.1 = (f32[4096,256]{0,1:T(8,128)S(1)}, f32[4096,256]{0,1:T(8,128)}, u32[]{:S(2)}) copy-start(f32[4096,256]{0,1:T(8,128)} %get-tuple-element.273) | copy-start | bytes 12582916 | tf_op jit(solution)/shard_map/while
  104.7 4.5 %copy-start.1 = (f32[4096,256]{0,1:T(8,128)S(1)}, f32[4096,256]{0,1:T(8,128)}, u32[]{:S(2)}) copy-start(f32[4096,256]{0,1:T(8,128)} %get-tuple-element.273) | copy-start | bytes 12582916 | tf_op jit(solution)/shard_map/while
  123.3 4.5 %copy-start.1 = (f32[4096,256]{0,1:T(8,128)S(1)}, f32[4096,256]{0,1:T(8,128)}, u32[]{:S(2)}) copy-start(f32[4096,256]{0,1:T(8,128)} %get-tuple-element.273) | copy-start | bytes 12582916 | tf_op jit(solution)/shard_map/while
  142.0 4.5 %copy-start.1 = (f32[4096,256]{0,1:T(8,128)S(1)}, f32[4096,256]{0,1:T(8,128)}, u32[]{:S(2)}) copy-start(f32[4096,256]{0,1:T(8,128)} %get-tuple-element.273) | copy-start | bytes 12582916 | tf_op jit(solution)/shard_map/while
  179.3 4.5 %copy-start.1 = (f32[4096,256]{0,1:T(8,128)S(1)}, f32[4096,256]{0,1:T(8,128)}, u32[]{:S(2)}) copy-start(f32[4096,256]{0,1:T(8,128)} %get-tuple-element.273) | copy-start | bytes 12582916 | tf_op jit(solution)/shard_map/while
  235.8 18.0 %all-to-all-start.3 = ((f32[32,1,512]{2,1,0:T(1,128)}), f32[32,1,512]{2,1,0:T(1,128)S(1)}, u32[]{:S(2)}, u32[]{:S(2)}) async-start(f32[32,1,512]{2,1,0:T(1,128)} %bitcast.20), calls=%async_computation.3 | async-start | bytes 131072 | tf_op jit(solution)/shard_map/all_to_all | solution.py:155
  253.9 8.4 %copy-start.5 = (s32[32,8]{0,1:T(8,128)S(1)}, s32[32,8]{0,1:T(8,128)}, u32[]{:S(2)}) copy-start(s32[32,8]{0,1:T(8,128)} %param.30) | copy-start | bytes 3076
  253.9 59.8 %all-to-all-start.1 = ((f32[32,256,128]{2,1,0:T(8,128)}), f32[32,256,128]{2,1,0:T(8,128)}, u32[]{:S(2)}, u32[]{:S(2)}) async-start(f32[32,256,128]{2,1,0:T(8,128)} %reshape.611), calls=%async_computation.1 | async-start | bytes 8388608 | tf_op jit(solution)/shard_map/all_to_all | solution.py:162
  261.6 92.6 %reduce-scatter.2.cloned.1.call-start = ((), (), s32[]{:S(2)}) async-start(), calls=%async_computation.8 | async-start | bytes 589824 | tf_op jit(solution)/shard_map/reduce_scatter | solution.py:206
  287.2 30.4 %copy-start.4 = (bf16[128,1024]{1,0:T(8,128)(2,1)S(1)}, bf16[128,1024]{1,0:T(8,128)(2,1)}, u32[]{:S(2)}) copy-start(bf16[128,1024]{1,0:T(8,128)(2,1)} %param.22) | copy-start | bytes 786436
  287.2 68.0 %copy-start.6 = (f32[1024]{0:T(1024)S(1)}, f32[1024]{0:T(1024)}, u32[]{:S(2)}) copy-start(f32[1024]{0:T(1024)} %param.23) | copy-start | bytes 12292
  358.6 29.2 %all-to-all-start.4 = ((bf16[32,12,1024]{2,1,0:T(8,128)(2,1)}), bf16[32,12,1024]{2,1,0:T(8,128)(2,1)S(1)}, u32[]{:S(2)}, u32[]{:S(2)}) async-start(bf16[32,12,1024]{2,1,0:T(8,128)(2,1)} %broadcast_select_fusion), calls=%async_computation.5 | async-start | bytes 2097152 | tf_op jit(solution)/shard_map/all_to_all | solution.py:228
  390.7 8.5 %copy-start.7 = (f32[32,8]{0,1:T(8,128)S(1)}, f32[32,8]{0,1:T(8,128)}, u32[]{:S(2)}) copy-start(f32[32,8]{0,1:T(8,128)} %param.31) | copy-start | bytes 3076
  394.5 21.6 %all-to-all-start.5 = ((bf16[32,12,1024]{2,1,0:T(8,128)(2,1)}), bf16[32,12,1024]{2,1,0:T(8,128)(2,1)}, u32[]{:S(2)}, u32[]{:S(2)}) async-start(bf16[32,12,1024]{2,1,0:T(8,128)(2,1)} %reshape.620), calls=%async_computation.6 | async-start | bytes 2097152 | tf_op jit(solution)/shard_map/all_to_all | solution.py:237
  (3 other events, 13.6 us)
Sparse Core Ops, SparseCore 0:
  28.8 56.0 all-gather.1
  318.8 35.2 reduce-scatter.1
